TPU v7x, 32 devices: a whole 2x2x4 slice. The times are simulated.
32 devices in a mesh: slab: 4 (over x, core), grp: 8 (over z, y).
Axes of the slice: x: 2, y: 2, z: 4, core: 2. Of those that a mesh axis runs over, the one named last changes fastest.
Arguments:
- raw_frames: bfloat16 [256, 48, 10752], P('grp', 'slab'), may hold values from -700 to 700
- mask_index: int32 [57344], P(('slab', 'grp')), may hold values from 0 to 516095, as said below
- subspace: bfloat16 [1200, 57344], P(None, ('slab', 'grp')), may hold values from -6 to 6
- rotation: bfloat16 [1456, 1200], replicated, may hold values from -0.15625 to 0.15625
Outputs:
- gram: float32 [1456, 1456], P('grp')
- new_subspace: bfloat16 [1200, 57344], P(None, ('slab', 'grp'))
Inputs may be any that keep to these rules, and one draw needn't show every extreme that they name: `mask_index`: entries are distinct flat grid positions that come in runs of 128 consecutive positions, each run starting at a multiple of 128; the 14336 entries of aligned block s lie in z planes s * 12 to (s + 1) * 12 - 1 and rise within the block; the first 3584 of a block lie in its lowest 3 planes, the last 3584 in its highest 3 planes, the others in the planes between.
All inputs are finite; a program needn't handle non-finite values.
Results may differ from a plain program's by a relative error of at most 0.006.
Values may be sent and summed in bfloat16 or wider, within the bound.
A program may use at most 192 MiB of HBM per device.

v0:
```python
import math
import jax
import jax.numpy as jnp
from jax import lax
from jax.sharding import PartitionSpec as P

NX = 96
RUN = 128
RAD = 3
K = 1200
smooth_sigma = 1.0617
epsilon = 1e-06


def padded_2(cells, sides, width):
    for axis, dim in sides:
        count = lax.axis_size(axis)
        ends = count - 1
        head = lax.slice_in_dim(cells, 0, width, axis=dim)
        tail = lax.slice_in_dim(cells, cells.shape[dim] - width, cells.shape[dim], axis=dim)
        cells = jnp.concatenate(
            [
                lax.ppermute(tail, axis, [(i, (i + 1) % count) for i in range(ends)]),
                cells,
                lax.ppermute(head, axis, [((i + 1) % count, i) for i in range(ends)]),
            ],
            axis=dim,
        )
    return cells


def tap_weights():
    unscaled = [
        math.exp(-offset * offset / (2.0 * smooth_sigma * smooth_sigma))
        for offset in range(-RAD, RAD + 1)
    ]
    summed = sum(unscaled)
    return [weight / summed for weight in unscaled]


def along_rows(volume):
    weights = tap_weights()
    extent = volume.shape[-1]
    column = lax.broadcasted_iota(jnp.int32, (extent,), 0) % NX
    padded = jnp.pad(volume, [(0, 0)] * (volume.ndim - 1) + [(RAD, RAD)])
    summed = jnp.zeros(volume.shape, jnp.float32)
    for offset in range(-RAD, RAD + 1):
        shifted = lax.slice_in_dim(
            padded, RAD + offset, RAD + offset + extent, axis=volume.ndim - 1
        )
        inside = (column + offset >= 0) & (column + offset < NX)
        summed = summed + weights[offset + RAD] * jnp.where(inside, shifted, 0.0)
    return summed


def along_columns(volume):
    weights = tap_weights()
    extent = volume.shape[-1]
    reach_cells = RAD * NX
    padded = jnp.pad(volume, [(0, 0)] * (volume.ndim - 1) + [(reach_cells, reach_cells)])
    summed = jnp.zeros(volume.shape, jnp.float32)
    for offset in range(-RAD, RAD + 1):
        begin = reach_cells + offset * NX
        shifted = lax.slice_in_dim(padded, begin, begin + extent, axis=volume.ndim - 1)
        summed = summed + weights[offset + RAD] * shifted
    return summed


def along_depth(padded, slab_depth):
    weights = tap_weights()
    summed = None
    for offset in range(-RAD, RAD + 1):
        shifted = lax.slice_in_dim(
            padded, RAD + offset, RAD + offset + slab_depth, axis=padded.ndim - 2
        )
        term = weights[offset + RAD] * shifted
        summed = term if summed is None else summed + term
    return summed


def pick_columns(matrix, wanted):
    row_total = matrix.shape[0]
    blocked = matrix.reshape(row_total, matrix.shape[1] // RUN, RUN)
    run_starts = wanted.reshape(-1, RUN)[:, 0] // RUN
    picked_runs = jnp.take(blocked, run_starts, axis=1)
    return picked_runs.reshape(row_total, wanted.shape[0])


def body(raw_frames, mask_index, subspace, rotation):
    frames_here = raw_frames.shape[0]
    slab_depth = raw_frames.shape[1]
    extent = raw_frames.shape[2]
    per_device = subspace.shape[1]
    group_count = lax.axis_size("grp")
    masked = per_device * lax.axis_size("slab") * group_count
    positions = lax.all_gather(mask_index, "grp", axis=0, tiled=True) - lax.axis_index("slab") * (
        slab_depth * extent
    )
    padded = padded_2(raw_frames, (("slab", 1),), RAD)
    planar = along_columns(along_rows(padded.astype(jnp.float32)))
    smoothed = (
        along_depth(planar, slab_depth)
        .reshape(frames_here, slab_depth * extent)
        .astype(jnp.bfloat16)
    )
    picked = pick_columns(smoothed, positions)
    regrouped = lax.all_to_all(picked, "grp", split_axis=1, concat_axis=0, tiled=True)
    frame_count = regrouped.shape[0]
    subject_frames = frame_count // 2
    halves = regrouped.astype(jnp.float32).reshape(2, subject_frames, per_device)
    centered = (halves - jnp.mean(halves, axis=1, keepdims=True)).astype(jnp.bfloat16)
    order_rows = K + frame_count
    stacked = jnp.concatenate([subspace, centered.reshape(frame_count, per_device)], 0)
    widened = centered.astype(jnp.float32)
    power = lax.psum(jnp.sum(widened * widened, axis=(1, 2)), ("slab", "grp"))
    rows_here = order_rows // group_count
    first_row = lax.axis_index("grp") * rows_here
    gram_raw = lax.psum(
        jnp.dot(stacked, stacked.T, preferred_element_type=jnp.float32), ("slab", "grp")
    )
    owned = lax.dynamic_slice_in_dim(gram_raw, first_row, rows_here, 0)
    scales = lax.rsqrt(power / (masked * subject_frames) + epsilon)
    row_scale = jnp.concatenate([jnp.ones((K,), jnp.float32), jnp.repeat(scales, subject_frames)])
    owned_scale = lax.dynamic_slice_in_dim(row_scale, first_row, rows_here, 0)
    gram_rows = owned * (owned_scale[:, None] * row_scale[None, :]) / masked
    contract = (((0,), (0,)), ((), ()))
    from_basis = lax.dot_general(
        rotation[:K], subspace, contract, preferred_element_type=jnp.float32
    )
    from_first = lax.dot_general(
        rotation[K : K + subject_frames], centered[0], contract, preferred_element_type=jnp.float32
    )
    from_second = lax.dot_general(
        rotation[K + subject_frames :], centered[1], contract, preferred_element_type=jnp.float32
    )
    new_subspace = (from_basis + scales[0] * from_first + scales[1] * from_second).astype(
        jnp.bfloat16
    )
    return (gram_rows, new_subspace)


def solution(mesh):
    placed = (P("grp", "slab", None), P(("slab", "grp")), P(None, ("slab", "grp")), P())
    return jax.shard_map(
        body,
        mesh=mesh,
        in_specs=placed,
        out_specs=(P("grp", None), P(None, ("slab", "grp"))),
        check_vma=False,
    )
```

profile of v0, /device:TPU:0, one launch (start us, length us, event | category | flops | bytes accessed | tf_op | source)
XLA Modules:
  0.0 511.2 jit_solution(89150723595462847)
XLA Ops:
  7.2 0.0 all-reduce.5.cloned.1.call-start
  7.2 4.5 fusion.61
  11.7 2.5 collective-permute-start
  14.2 1.3 collective-permute-start.1
  15.5 0.7 reshape.63
  16.2 31.9 %all-gather = s32[8,1,1792]{2,1,0:T(1,128)S(1)} all-gather(s32[1,1,1792]{2,1,0:T(1,128)S(1)} %reshape.63), channel_id=1, replica_groups=mesh['slab'=4,'grp'=8] {'grp'}, dimensions={0}, use_global_device_ids=true | all-gather | bytes 64512 | tf_op jit(solution)/shard_map/all_gather | solution.py:96
  48.1 0.1 and_reduce_fusion
  48.2 0.1 broadcast_in_dim.55
  48.3 0.1 copy.22
  48.4 0.1 reduce.5
  48.8 0.1 broadcast_bitcast_fusion
  48.8 0.0 collective-permute-done
  48.9 0.0 collective-permute-done.1
  48.9 12.9 %maximum_convert_fusion = f32[32,18,10752]{2,0,1:T(8,128)} fusion(bf16[32,3,10752]{2,0,1:T(8,128)(2,1)} %collective-permute-done.1, bf16[32,12,10752]{2,0,1:T(8,128)(2,1)} %param.4, bf16[32,3,10752]{2,0,1:T(8,128)(2,1)S(1)} %collective-permute-done), kind=kLoop, calls=%fused_computation.29 | loop fusion | flops 18579456 | bytes 37158912 | tf_op jit(solution)/shard_map/convert_element_type | solution.py:100
  61.8 64.2 %multiply_add_fusion.1 = f32[32,18,10752]{2,0,1:T(8,128)} fusion(f32[32,18,10752]{2,0,1:T(8,128)} %maximum_convert_fusion, pred[10752]{0:T(1024)(128)(4,1)S(1)} %get-tuple-element.8, pred[10752]{0:T(1024)(128)(4,1)S(1)} %get-tuple-element.9, pred[10752]{0:T(1024)(128)(4,1)S(1)} %get-tuple-element.10, pred[10752]{0:T(1024)(128)(4,1)S(1)} %fusion.58, ...), kind=kLoop, calls=%fused_computation.7 | loop fusion | flops 123863040 | bytes 49620480 | tf_op jit(solution)/shard_map/add | solution.py:52
  125.9 64.0 %multiply_add_fusion = f32[32,18,10752]{2,0,1:T(8,128)} fusion(f32[32,18,10752]{2,0,1:T(8,128)} %multiply_add_fusion.1), kind=kLoop, calls=%fused_computation.1 | loop fusion | flops 80510976 | bytes 49545216 | tf_op jit(solution)/shard_map/add | solution.py:65
  189.9 40.4 %fusion.9 = bf16[32,12,10752]{2,0,1:T(8,128)(2,1)} fusion(f32[32,18,10752]{2,0,1:T(8,128)} %multiply_add_fusion), kind=kLoop, calls=%fused_computation.17 | loop fusion | flops 57802752 | bytes 123863040 | tf_op jit(solution)/shard_map/convert_element_type | solution.py:104
  230.3 12.2 %copy.23 = bf16[32,12,10752]{2,1,0:T(8,128)(2,1)} copy(bf16[32,12,10752]{2,0,1:T(8,128)(2,1)} %fusion.9) | data formatting | bytes 16515072 | tf_op jit(solution)/shard_map/convert_element_type | solution.py:104
  242.5 18.6 %convert_element_type.54 = bf16[32,1008,128]{2,1,0:T(8,128)(2,1)} reshape(bf16[32,12,10752]{2,1,0:T(8,128)(2,1)} %copy.23) | data formatting | bytes 16515072 | tf_op jit(solution)/shard_map/convert_element_type | solution.py:104
  261.0 8.6 %copy.24 = bf16[32,1008,128]{2,0,1:T(8,128)(2,1)} copy(bf16[32,1008,128]{2,1,0:T(8,128)(2,1)} %convert_element_type.54) | data formatting | bytes 16515072 | tf_op jit(solution)/shard_map/convert_element_type | solution.py:104
  269.7 4.1 gather_fusion
  273.8 0.4 copy.25
  274.1 1.0 gather.7
  275.1 0.1 broadcast_select_fusion
  275.2 0.2 copy.26
  275.4 24.6 %all_to_all.10 = bf16[32,8,1792]{2,0,1:T(8,128)(2,1)S(1)} all-to-all(bf16[32,8,1792]{2,0,1:T(8,128)(2,1)S(1)} %copy.26), channel_id=1, replica_groups=mesh['slab'=4,'grp'=8] {'grp'}, dimensions={1} | all-to-all | bytes 1835008 | tf_op jit(solution)/shard_map/all_to_all | solution.py:107
  300.1 0.2 bitcast_reduce_fusion
  300.4 0.2 fusion.24
  300.5 14.3 %fusion.19 = f32[1456,1456]{1,0:T(8,128)} fusion(bf16[256,1792]{1,0:T(8,128)(2,1)S(1)} %fusion.24, bf16[1200,1792]{1,0:T(8,128)(2,1)} %param.6), kind=kOutput, calls=%fused_computation.37 | convolution fusion | flops 7608287232 | bytes 13698048 | tf_op jit(solution)/shard_map/dot_general | solution.py:119
  314.9 0.0 all-reduce.5.cloned.1.call-update
  314.9 0.4 multiply_reduce_fusion
  315.3 0.1 reduce_sum.36
  315.4 0.1 reduce_sum.37
  315.5 40.8 %psum.15 = f32[2]{0:T(128)S(1)} all-reduce(f32[2]{0:T(128)S(1)} %reduce_sum.37), channel_id=1, replica_groups=mesh['slab'=4,'grp'=8] {'slab','grp'}, use_global_device_ids=true, to_apply=%region_5.6 | all-reduce | flops 2 | bytes 16 | tf_op jit(solution)/shard_map/psum | solution.py:115
  356.3 0.1 broadcast_bitcast_fusion.1
  356.4 0.1 concatenate.11
  356.5 0.1 convert_element_type.69
  356.6 0.1 pad_dynamic-slice_fusion
  356.7 0.6 fusion.62
  357.3 0.1 subtract_convert_fusion
  357.4 0.0 copy-start
  357.4 3.5 fusion.16
  360.9 3.1 fusion.17
  364.0 0.0 copy-done
  364.0 9.7 %fusion.18 = bf16[1200,1792]{1,0:T(8,128)(2,1)} fusion(f32[1200,1792]{1,0:T(8,128)S(1)} %fusion.17, f32[1200,1792]{1,0:T(8,128)S(1)} %fusion.16, bf16[1200,1792]{1,0:T(8,128)(2,1)} %param.6, bf16[1456,1200]{0,1:T(8,128)(2,1)S(1)} %copy-done), kind=kOutput, calls=%fused_computation.36 | convolution fusion | flops 5167411200 | bytes 28876800 | tf_op jit(solution)/shard_map/dot_general | solution.py:127
  373.7 128.2 %all-reduce.5.cloned.1.call-done = f32[1456,1456]{1,0:T(8,128)} async-done(((f32[1456,1456]{1,0:T(8,128)}), f32[1456,1456]{1,0:T(8,128)}) %all-reduce.5.cloned.1.call-update) | async-done | bytes 8479760 | tf_op jit(solution)/shard_map/psum | solution.py:118
  501.9 2.5 multiply_multiply_fusion
  (12 shorter events, 0.3 us)
Async XLA Ops:
  7.2 494.8 %all-reduce.5.cloned.1.call-start = ((), (), s32[]{:S(2)}) async-start(), calls=%async_computation.1 | async-start | bytes 17891328 | tf_op jit(solution)/shard_map/psum | solution.py:118
  11.7 37.2 %collective-permute-start = (bf16[32,3,10752]{2,0,1:T(8,128)(2,1)}, bf16[32,3,10752]{2,0,1:T(8,128)(2,1)S(1)}, u32[]{:S(2)}, u32[]{:S(2)}) collective-permute-start(bf16[32,3,10752]{2,0,1:T(8,128)(2,1)} %get-tuple-element.4), channel_id=1, source_target_pairs={{0,8},{8,16},{16,24},{1,9},{9,17},{17,25},{2,10},{10,18},{18,26},{... | collective-permute-start | bytes 6193160 | tf_op jit(solution)/shard_map/ppermute | solution.py:23
  14.2 34.6 %collective-permute-start.1 = (bf16[32,3,10752]{2,0,1:T(8,128)(2,1)}, bf16[32,3,10752]{2,0,1:T(8,128)(2,1)}, u32[]{:S(2)}, u32[]{:S(2)}) collective-permute-start(bf16[32,3,10752]{2,0,1:T(8,128)(2,1)} %get-tuple-element.5), channel_id=1, source_target_pairs={{8,0},{16,8},{24,16},{9,1},{17,9},{25,17},{10,2},{18,10},{26,18},{... | collective-permute-start | bytes 6193160 | tf_op jit(solution)/shard_map/ppermute | solution.py:25
  357.4 6.6 %copy-start = (bf16[1456,1200]{0,1:T(8,128)(2,1)S(1)}, bf16[1456,1200]{0,1:T(8,128)(2,1)}, u32[]{:S(2)}) copy-start(bf16[1456,1200]{0,1:T(8,128)(2,1)} %param.7) | copy-start | bytes 10483204
Sparse Core Ops, SparseCore 0:
  315.0 186.8 all-reduce.4
where the time goes:
time: 512 us; the launch traced here: 511 us
  other arithmetic  186 us (36%)
  waiting for transfers between devices  128 us (25%)
  blocking collectives  97.3 us (19%)
  local copies, waits for them, and re-layouts  51.4 us (10%)
  matrix products  30.6 us (6%)
  between operations  14.2 us (3%)
    psum x1, waiting for transfers between devices, body(): lax.psum(jnp.dot(stacked, stacked.T, preferred_element_type=jnp.float32),...  128 us
    add x1, other arithmetic, along_rows(): summed = summed + weights[offset + RAD] * jnp.where(inside, shifted, 0.0)  64.2 us
    add x1, other arithmetic, along_columns(): summed = summed + weights[offset + RAD] * shifted  64 us
    psum x1, blocking collectives, body(): power = lax.psum(jnp.sum(widened * widened, axis=(1, 2)), ('slab', 'grp'))  40.8 us
    convert_element_type x1, other arithmetic, body(): smoothed = along_depth(planar, slab_depth).reshape(frames_here, slab_dept...  40.4 us
    convert_element_type x3, local copies, waits for them, and re-layouts, body(): smoothed = along_depth(planar, slab_depth).reshape(frames_here, slab_dept...  39.4 us
    all_gather x1, blocking collectives, body(): lax.all_gather(mask_index, 'grp', axis=0, tiled=True)  31.9 us
    all_to_all x1, blocking collectives, body(): lax.all_to_all(picked, 'grp', split_axis=1, concat_axis=0, tiled=True)  24.6 us
  transfers between devices with their start and end apart: 3, of which 1 were waited for; matrix products, arithmetic and copies ran while one was open for 4% of the time, Pallas kernels for 0%

commit v1 on v0

--- a/solution.py
+++ b/solution.py
@@ -112,7 +112,9 @@
     order_rows = K + frame_count
     stacked = jnp.concatenate([subspace, centered.reshape(frame_count, per_device)], 0)
     widened = centered.astype(jnp.float32)
-    power = lax.psum(jnp.sum(widened * widened, axis=(1, 2)), ("slab", "grp"))
+    power = jnp.sum(
+        lax.all_gather(jnp.sum(widened * widened, axis=(1, 2)), ("slab", "grp")), axis=0
+    )
     rows_here = order_rows // group_count
     first_row = lax.axis_index("grp") * rows_here
     gram_raw = lax.psum(

time: 512 us -> 512 us (level)
    psum x1 -> x0, blocking collectives: 40.8 us -> none  [body(): power = lax.psum(jnp.sum(widened * widened, axis=(1, 2)), ('slab', 'grp'))]
    unnamed x0 -> x1, blocking collectives: none -> 40.7 us
where the time goes in v1:
time: 512 us; the launch traced here: 511 us
  other arithmetic  186 us (36%)
  waiting for transfers between devices  128 us (25%)
  blocking collectives  97.2 us (19%)
  local copies, waits for them, and re-layouts  51.8 us (10%)
  matrix products  30.6 us (6%)
  between operations  14.3 us (3%)
    psum x1, waiting for transfers between devices, body(): lax.psum(jnp.dot(stacked, stacked.T, preferred_element_type=jnp.float32),...  128 us
    add x1, other arithmetic, along_rows(): summed = summed + weights[offset + RAD] * jnp.where(inside, shifted, 0.0)  64.2 us
    add x1, other arithmetic, along_columns(): summed = summed + weights[offset + RAD] * shifted  64 us
    unnamed x1, blocking collectives  40.7 us
    convert_element_type x1, other arithmetic, body(): smoothed = along_depth(planar, slab_depth).reshape(frames_here, slab_dept...  40.4 us
    convert_element_type x3, local copies, waits for them, and re-layouts, body(): smoothed = along_depth(planar, slab_depth).reshape(frames_here, slab_dept...  39.4 us
    all_gather x1, blocking collectives, body(): lax.all_gather(mask_index, 'grp', axis=0, tiled=True)  31.9 us
    all_to_all x1, blocking collectives, body(): lax.all_to_all(picked, 'grp', split_axis=1, concat_axis=0, tiled=True)  24.6 us
  transfers between devices with their start and end apart: 3, of which 1 were waited for; matrix products, arithmetic and copies ran while one was open for 4% of the time, Pallas kernels for 0%

profile of v1, /device:TPU:0, one launch (start us, length us, event | category | flops | bytes accessed | tf_op | source)
XLA Modules:
  0.0 511.2 jit_solution(691329496252527122)
XLA Ops:
  7.2 0.0 all-reduce.6.cloned.1.call-start
  7.2 4.5 fusion.61
  11.7 2.5 collective-permute-start
  14.2 1.3 collective-permute-start.1
  15.5 0.7 reshape.66
  16.2 31.9 %all-gather.1 = s32[8,1,1792]{2,1,0:T(1,128)S(1)} all-gather(s32[1,1,1792]{2,1,0:T(1,128)S(1)} %reshape.66), channel_id=1, replica_groups=mesh['slab'=4,'grp'=8] {'grp'}, dimensions={0}, use_global_device_ids=true | all-gather | bytes 64512 | tf_op jit(solution)/shard_map/all_gather | solution.py:96
  48.1 0.1 and_reduce_fusion
  48.2 0.1 broadcast_in_dim.55
  48.3 0.1 copy.22
  48.4 0.1 reduce.5
  48.8 0.1 broadcast_bitcast_fusion
  48.8 0.0 collective-permute-done
  48.9 0.0 collective-permute-done.1
  48.9 12.9 %maximum_convert_fusion = f32[32,18,10752]{2,0,1:T(8,128)} fusion(bf16[32,3,10752]{2,0,1:T(8,128)(2,1)} %collective-permute-done.1, bf16[32,12,10752]{2,0,1:T(8,128)(2,1)} %param.4, bf16[32,3,10752]{2,0,1:T(8,128)(2,1)S(1)} %collective-permute-done), kind=kLoop, calls=%fused_computation.29 | loop fusion | flops 18579456 | bytes 37158912 | tf_op jit(solution)/shard_map/convert_element_type | solution.py:100
  61.8 64.2 %multiply_add_fusion.1 = f32[32,18,10752]{2,0,1:T(8,128)} fusion(f32[32,18,10752]{2,0,1:T(8,128)} %maximum_convert_fusion, pred[10752]{0:T(1024)(128)(4,1)S(1)} %get-tuple-element.8, pred[10752]{0:T(1024)(128)(4,1)S(1)} %get-tuple-element.9, pred[10752]{0:T(1024)(128)(4,1)S(1)} %get-tuple-element.10, pred[10752]{0:T(1024)(128)(4,1)S(1)} %fusion.58, ...), kind=kLoop, calls=%fused_computation.7 | loop fusion | flops 123863040 | bytes 49620480 | tf_op jit(solution)/shard_map/add | solution.py:52
  125.9 64.0 %multiply_add_fusion = f32[32,18,10752]{2,0,1:T(8,128)} fusion(f32[32,18,10752]{2,0,1:T(8,128)} %multiply_add_fusion.1), kind=kLoop, calls=%fused_computation.1 | loop fusion | flops 80510976 | bytes 49545216 | tf_op jit(solution)/shard_map/add | solution.py:65
  189.9 40.4 %fusion.9 = bf16[32,12,10752]{2,0,1:T(8,128)(2,1)} fusion(f32[32,18,10752]{2,0,1:T(8,128)} %multiply_add_fusion), kind=kLoop, calls=%fused_computation.17 | loop fusion | flops 57802752 | bytes 123863040 | tf_op jit(solution)/shard_map/convert_element_type | solution.py:104
  230.3 12.2 %copy.23 = bf16[32,12,10752]{2,1,0:T(8,128)(2,1)} copy(bf16[32,12,10752]{2,0,1:T(8,128)(2,1)} %fusion.9) | data formatting | bytes 16515072 | tf_op jit(solution)/shard_map/convert_element_type | solution.py:104
  242.5 18.6 %convert_element_type.54 = bf16[32,1008,128]{2,1,0:T(8,128)(2,1)} reshape(bf16[32,12,10752]{2,1,0:T(8,128)(2,1)} %copy.23) | data formatting | bytes 16515072 | tf_op jit(solution)/shard_map/convert_element_type | solution.py:104
  261.0 8.6 %copy.24 = bf16[32,1008,128]{2,0,1:T(8,128)(2,1)} copy(bf16[32,1008,128]{2,1,0:T(8,128)(2,1)} %convert_element_type.54) | data formatting | bytes 16515072 | tf_op jit(solution)/shard_map/convert_element_type | solution.py:104
  269.7 4.1 gather_fusion
  273.8 0.4 copy.25
  274.1 1.0 gather.7
  275.1 0.1 broadcast_select_fusion
  275.2 0.2 copy.26
  275.4 24.6 %all_to_all.10 = bf16[32,8,1792]{2,0,1:T(8,128)(2,1)S(1)} all-to-all(bf16[32,8,1792]{2,0,1:T(8,128)(2,1)S(1)} %copy.26), channel_id=1, replica_groups=mesh['slab'=4,'grp'=8] {'grp'}, dimensions={1} | all-to-all | bytes 1835008 | tf_op jit(solution)/shard_map/all_to_all | solution.py:107
  300.1 0.2 bitcast_reduce_fusion
  300.4 0.2 fusion.24
  300.5 14.3 %fusion.19 = f32[1456,1456]{1,0:T(8,128)} fusion(bf16[256,1792]{1,0:T(8,128)(2,1)S(1)} %fusion.24, bf16[1200,1792]{1,0:T(8,128)(2,1)} %param.6), kind=kOutput, calls=%fused_computation.37 | convolution fusion | flops 7608287232 | bytes 13698048 | tf_op jit(solution)/shard_map/dot_general | solution.py:121
  314.9 0.0 all-reduce.6.cloned.1.call-update
  314.9 0.4 multiply_reduce_fusion
  315.3 0.1 reduce_sum.45
  315.4 0.1 reduce_sum.46
  315.5 0.2 dynamic-update-slice
  315.8 40.7 %all-reduce.3 = f32[64]{0:T(128)S(1)} all-reduce(f32[64]{0:T(128)S(1)} %dynamic-update-slice), channel_id=2, replica_groups=mesh['slab'=4,'grp'=8] {'slab','grp'}, use_global_device_ids=true, to_apply=%add.3 | all-reduce | flops 64 | bytes 512
  356.5 0.1 reshape.63
  356.6 0.1 broadcast_bitcast_fusion.1
  356.7 0.1 concatenate.11
  356.8 0.2 convert_element_type.69
  356.9 0.1 pad_dynamic-slice_fusion
  357.0 0.6 fusion.62
  357.6 0.1 subtract_convert_fusion
  357.7 0.0 copy-start
  357.7 3.5 fusion.16
  361.3 3.1 fusion.17
  364.3 0.0 copy-done
  364.4 9.7 %fusion.18 = bf16[1200,1792]{1,0:T(8,128)(2,1)} fusion(f32[1200,1792]{1,0:T(8,128)S(1)} %fusion.17, f32[1200,1792]{1,0:T(8,128)S(1)} %fusion.16, bf16[1200,1792]{1,0:T(8,128)(2,1)} %param.6, bf16[1456,1200]{0,1:T(8,128)(2,1)S(1)} %copy-done), kind=kOutput, calls=%fused_computation.36 | convolution fusion | flops 5167411200 | bytes 28876800 | tf_op jit(solution)/shard_map/dot_general | solution.py:129
  374.0 127.9 %all-reduce.6.cloned.1.call-done = f32[1456,1456]{1,0:T(8,128)} async-done(((f32[1456,1456]{1,0:T(8,128)}), f32[1456,1456]{1,0:T(8,128)}) %all-reduce.6.cloned.1.call-update) | async-done | bytes 8479760 | tf_op jit(solution)/shard_map/psum | solution.py:120
  501.9 2.5 multiply_multiply_fusion
  (14 shorter events, 0.3 us)
Async XLA Ops:
  7.2 494.8 %all-reduce.6.cloned.1.call-start = ((), (), s32[]{:S(2)}) async-start(), calls=%async_computation.1 | async-start | bytes 17891328 | tf_op jit(solution)/shard_map/psum | solution.py:120
  11.7 37.2 %collective-permute-start = (bf16[32,3,10752]{2,0,1:T(8,128)(2,1)}, bf16[32,3,10752]{2,0,1:T(8,128)(2,1)S(1)}, u32[]{:S(2)}, u32[]{:S(2)}) collective-permute-start(bf16[32,3,10752]{2,0,1:T(8,128)(2,1)} %get-tuple-element.4), channel_id=1, source_target_pairs={{0,8},{8,16},{16,24},{1,9},{9,17},{17,25},{2,10},{10,18},{18,26},{... | collective-permute-start | bytes 6193160 | tf_op jit(solution)/shard_map/ppermute | solution.py:23
  14.2 34.6 %collective-permute-start.1 = (bf16[32,3,10752]{2,0,1:T(8,128)(2,1)}, bf16[32,3,10752]{2,0,1:T(8,128)(2,1)}, u32[]{:S(2)}, u32[]{:S(2)}) collective-permute-start(bf16[32,3,10752]{2,0,1:T(8,128)(2,1)} %get-tuple-element.5), channel_id=1, source_target_pairs={{8,0},{16,8},{24,16},{9,1},{17,9},{25,17},{10,2},{18,10},{26,18},{... | collective-permute-start | bytes 6193160 | tf_op jit(solution)/shard_map/ppermute | solution.py:25
  357.7 6.6 %copy-start = (bf16[1456,1200]{0,1:T(8,128)(2,1)S(1)}, bf16[1456,1200]{0,1:T(8,128)(2,1)}, u32[]{:S(2)}) copy-start(bf16[1456,1200]{0,1:T(8,128)(2,1)} %param.7) | copy-start | bytes 10483204
Sparse Core Ops, SparseCore 0:
  315.0 186.8 all-reduce.5
